TPU v7x, 256 devices: a whole 4x4x8 slice. The times are simulated.
256 devices in a mesh: grp: 8 (over x, core), dev: 32 (over y, z).
Axes of the slice: x: 4, y: 4, z: 8, core: 2. Of those that a mesh axis runs over, the one named last changes fastest.
Arguments:
- tensor_slab: bfloat16 [512, 512, 64, 64], P(None, 'dev', 'grp'), may hold values from -400 to 400
- mode_factor: bfloat16 [512, 64], replicated, may hold values from -40 to 40
Outputs:
- triangle: float32 [512, 512], P('dev', 'grp')
All inputs are finite; a program needn't handle non-finite values.
Results may differ from a plain program's by a relative error of at most 0.00033.
Values may be sent and summed in bfloat16 or wider, within the bound.
A program may use at most 64 MiB of HBM per device.

v0:
```python
import jax
import jax.numpy as jnp
from jax import lax
from jax.sharding import PartitionSpec as P


def own_block(full_tri):
    order = full_tri.shape[0]
    row_count = order // lax.axis_size("dev")
    col_count = order // lax.axis_size("grp")
    row_start = lax.axis_index("dev") * row_count
    col_start = lax.axis_index("grp") * col_count
    return lax.dynamic_slice(full_tri, (row_start, col_start), (row_count, col_count))


def per_device(tensor_slab, mode_factor):
    row_width = tensor_slab.shape[0]
    local_cols = tensor_slab.shape[1]
    slab_depth = tensor_slab.shape[2]
    species = tensor_slab.shape[3]
    flat_slab = tensor_slab.reshape(row_width, local_cols * slab_depth * species)
    projected = lax.dot_general(
        mode_factor, flat_slab, (((0,), (0,)), ((), ())), preferred_element_type=jnp.float32
    )
    projected = projected.astype(jnp.bfloat16).reshape(
        mode_factor.shape[1], local_cols, slab_depth * species
    )
    regrouped = lax.all_to_all(projected, "dev", split_axis=0, concat_axis=1, tiled=True)
    gram_local = lax.dot_general(
        regrouped, regrouped, (((0, 2), (0, 2)), ((), ())), preferred_element_type=jnp.float32
    )
    row_total = mode_factor.shape[1] * slab_depth * species * lax.axis_size("grp")
    gram_local = gram_local / row_total
    gram_total = lax.psum(gram_local, ("grp", "dev"))
    return own_block(jnp.linalg.cholesky(gram_total).T)


def solution(mesh):
    in_specs = (P(None, "dev", "grp", None), P())
    out_specs = P("dev", "grp")
    return jax.shard_map(
        per_device, mesh=mesh, in_specs=in_specs, out_specs=out_specs, check_vma=False
    )
```

profile of v0, /device:TPU:2, one launch (start us, length us, event | category | flops | bytes accessed | tf_op | source)
XLA Modules:
  0.0 405.6 jit_solution(6353518399661913828)
XLA Ops:
  6.5 0.8 copy-done
  7.4 6.0 %convolution_convert_fusion = bf16[64,8192]{1,0:T(8,128)(2,1)S(1)} fusion(bf16[512,64]{0,1:T(8,128)(2,1)S(1)} %copy-done, bf16[512,8192]{0,1:T(8,128)(2,1)} %bitcast.37), kind=kOutput, calls=%fused_computation | convolution fusion | flops 537395200 | bytes 9502720 | tf_op jit(solution)/shard_map/dot_general | solution.py:22
  13.4 0.4 copy.14
  13.7 39.9 %all_to_all.18 = bf16[64,16,512]{2,1,0:T(8,128)(2,1)S(1)} all-to-all(bf16[64,16,512]{2,1,0:T(8,128)(2,1)S(1)} %bitcast.38), channel_id=1, replica_groups=mesh['grp'=8,'dev'=32] {'dev'}, dimensions={0} | all-to-all | bytes 2097152 | tf_op jit(solution)/shard_map/all_to_all | solution.py:28
  53.7 1.8 fusion
  55.5 255.8 %all-reduce.3.cloned.1.call-done = f32[512,512]{0,1:T(8,128)} async-done(((f32[512,512]{0,1:T(8,128)}), f32[512,512]{0,1:T(8,128)}) %all-reduce.3.cloned.1.call-update) | async-done | bytes 1048592 | tf_op jit(solution)/shard_map/psum | solution.py:34
  311.3 1.6 copy.5
  312.9 1.4 fusion.1
  314.4 11.7 %cholesky.104 = f32[128,128]{1,0:T(8,128)S(1)} custom-call(f32[128,128]{1,0:T(8,128)S(1)} %cholesky.266), custom_call_target="Cholesky" | custom-call | tf_op jit(solution)/shard_map/jit(cholesky)/cholesky | solution.py:35
  326.1 9.8 %custom-call.27 = f32[1,128,128]{1,2,0:T(8,128)S(1)} custom-call(f32[1,128,128]{2,1,0:T(8,128)S(1)} %get-tuple-element.14), custom_call_target="InvertDiagBlocksLowerTriangular" | custom-call | tf_op jit(solution)/shard_map/jit(cholesky)/cholesky | solution.py:35
  335.9 0.4 fusion.4
  336.5 0.5 convolution_subtract_fusion
  337.1 11.7 %cholesky.217 = f32[128,128]{1,0:T(8,128)S(1)} custom-call(f32[128,128]{1,0:T(8,128)S(1)} %cholesky.270), custom_call_target="Cholesky" | custom-call | tf_op jit(solution)/shard_map/jit(cholesky)/cholesky | solution.py:35
  348.9 9.9 %custom-call.28 = f32[1,128,128]{1,2,0:T(8,128)S(1)} custom-call(f32[1,128,128]{2,1,0:T(8,128)S(1)} %get-tuple-element.11), custom_call_target="InvertDiagBlocksLowerTriangular" | custom-call | tf_op jit(solution)/shard_map/jit(cholesky)/cholesky | solution.py:35
  358.8 0.3 convolution_dynamic-update-slice_fusion
  359.1 0.4 convolution_subtract_fusion.1
  359.5 11.7 %cholesky.238 = f32[128,128]{1,0:T(8,128)S(1)} custom-call(f32[128,128]{1,0:T(8,128)S(1)} %cholesky.275), custom_call_target="Cholesky" | custom-call | tf_op jit(solution)/shard_map/jit(cholesky)/cholesky | solution.py:35
  371.2 0.7 compare_reduce_fusion.1
  372.0 9.8 %custom-call.29 = f32[1,128,128]{1,2,0:T(8,128)S(1)} custom-call(f32[1,128,128]{2,1,0:T(8,128)S(1)} %get-tuple-element.8), custom_call_target="InvertDiagBlocksLowerTriangular" | custom-call | tf_op jit(solution)/shard_map/jit(cholesky)/cholesky | solution.py:35
  382.0 0.4 convolution_subtract_fusion.2
  382.4 11.7 %cholesky.255 = f32[128,128]{1,0:T(8,128)S(1)} custom-call(f32[128,128]{1,0:T(8,128)S(1)} %convolution_subtract_fusion.2), custom_call_target="Cholesky" | custom-call | tf_op jit(solution)/shard_map/jit(cholesky)/cholesky | solution.py:35
  394.1 0.6 compare_reduce_fusion
  394.7 0.7 compare_reduce_fusion.2
  398.0 0.7 copy.9
  (16 shorter events, 0.8 us)
Async XLA Ops:
  6.5 0.8 copy-start
  6.5 304.8 %all-reduce.3.cloned.1.call-start = ((), (), s32[]{:S(2)}) async-start(), calls=%async_computation.1 | async-start | bytes 2097152 | tf_op jit(solution)/shard_map/psum | solution.py:34
Sparse Core Ops, SparseCore 0:
  55.6 255.6 all-reduce.2
where the time goes:
time: 406 us
  waiting for transfers between devices  256 us (63%)
  other arithmetic  80.1 us (20%)
  blocking collectives  39.9 us (10%)
  between operations  16.1 us (4%)
  matrix products  9.9 us (2%)
    psum x1, waiting for transfers between devices, per_device(): gram_total = lax.psum(gram_local, ('grp', 'dev'))  256 us
    another operation x14, other arithmetic, per_device(): return own_block(jnp.linalg.cholesky(gram_total).T)  78.6 us
    all_to_all x1, blocking collectives, per_device(): lax.all_to_all(projected, 'dev', split_axis=0, concat_axis=1, tiled=True)  39.9 us
  transfers between devices with their start and end apart: 1, of which 1 were waited for; matrix products, arithmetic and copies ran while one was open for 0% of the time, Pallas kernels for 0%

commit v1 on v0

--- a/solution.py
+++ b/solution.py
@@ -2,6 +2,8 @@
 import jax.numpy as jnp
 from jax import lax
 from jax.sharding import PartitionSpec as P
+
+_name_pieces_all = lambda u: lax.psum(lax.psum(u, "dev"), "grp")
 
 
 def own_block(full_tri):
@@ -31,7 +33,7 @@
     )
     row_total = mode_factor.shape[1] * slab_depth * species * lax.axis_size("grp")
     gram_local = gram_local / row_total
-    gram_total = lax.psum(gram_local, ("grp", "dev"))
+    gram_total = _name_pieces_all(gram_local)
     return own_block(jnp.linalg.cholesky(gram_total).T)
 
 

time: 406 us -> 365 us (0.90)
  waiting for transfers between devices: 256 us -> 212 us
    psum x1 -> x2, waiting for transfers between devices: 256 us -> 212 us  [_name_pieces_all = lambda u: lax.psum(lax.psum(u, 'dev'), 'grp')]
  transfers between devices with their start and end apart: 1 -> 2, of which waited for: 1 -> 2; matrix products, arithmetic and copies ran while one was open for 0% -> 0% of each run, Pallas kernels for 0% -> 0%
where the time goes in v1:
time: 365 us; the launch traced here: 362 us
  waiting for transfers between devices  212 us (58%)
  other arithmetic  80.1 us (22%)
  blocking collectives  39.9 us (11%)
  between operations  16.1 us (4%)
  matrix products  9.9 us (3%)
  local copies, waits for them, and re-layouts  3.77 us (1%)
    psum x2, waiting for transfers between devices, _name_pieces_all = lambda u: lax.psum(lax.psum(u, 'dev'), 'grp')  212 us
    another operation x14, other arithmetic, per_device(): return own_block(jnp.linalg.cholesky(gram_total).T)  78.6 us
    all_to_all x1, blocking collectives, per_device(): lax.all_to_all(projected, 'dev', split_axis=0, concat_axis=1, tiled=True)  39.9 us
  transfers between devices with their start and end apart: 2, of which 2 were waited for; matrix products, arithmetic and copies ran while one was open for 0% of the time, Pallas kernels for 0%

profile of v1, /device:TPU:2, one launch (start us, length us, event | category | flops | bytes accessed | tf_op | source)
XLA Modules:
  0.0 362.1 jit_solution(11102150243860336392)
XLA Ops:
  6.5 0.8 copy-done
  7.4 6.0 %convolution_convert_fusion = bf16[64,8192]{1,0:T(8,128)(2,1)S(1)} fusion(bf16[512,64]{0,1:T(8,128)(2,1)S(1)} %copy-done, bf16[512,8192]{0,1:T(8,128)(2,1)} %bitcast.37), kind=kOutput, calls=%fused_computation | convolution fusion | flops 537395200 | bytes 9502720 | tf_op jit(solution)/shard_map/dot_general | solution.py:24
  13.4 0.4 copy.14
  13.7 39.9 %all_to_all.18 = bf16[64,16,512]{2,1,0:T(8,128)(2,1)S(1)} all-to-all(bf16[64,16,512]{2,1,0:T(8,128)(2,1)S(1)} %bitcast.38), channel_id=1, replica_groups=mesh['grp'=8,'dev'=32] {'dev'}, dimensions={0} | all-to-all | bytes 2097152 | tf_op jit(solution)/shard_map/all_to_all | solution.py:30
  53.7 1.8 fusion
  55.8 147.0 %all-reduce.4.cloned.1.call-done = f32[512,512]{0,1:T(8,128)} async-done(((f32[512,512]{0,1:T(8,128)}), f32[512,512]{0,1:T(8,128)}) %all-reduce.4.cloned.1.call-update) | async-done | bytes 1048592 | tf_op jit(solution)/shard_map/psum | solution.py:6
  202.8 65.0 %all-reduce.6.cloned.1.call-done = f32[512,512]{0,1:T(8,128)} async-done(((f32[512,512]{0,1:T(8,128)}), f32[512,512]{0,1:T(8,128)}) %all-reduce.6.cloned.1.call-update) | async-done | bytes 1048592 | tf_op jit(solution)/shard_map/psum | solution.py:6
  267.8 1.6 copy.5
  269.4 1.4 fusion.1
  270.9 11.7 %cholesky.104 = f32[128,128]{1,0:T(8,128)S(1)} custom-call(f32[128,128]{1,0:T(8,128)S(1)} %cholesky.266), custom_call_target="Cholesky" | custom-call | tf_op jit(solution)/shard_map/jit(cholesky)/cholesky | solution.py:37
  282.6 9.8 %custom-call.27 = f32[1,128,128]{1,2,0:T(8,128)S(1)} custom-call(f32[1,128,128]{2,1,0:T(8,128)S(1)} %get-tuple-element.14), custom_call_target="InvertDiagBlocksLowerTriangular" | custom-call | tf_op jit(solution)/shard_map/jit(cholesky)/cholesky | solution.py:37
  292.4 0.4 fusion.4
  293.0 0.5 convolution_subtract_fusion
  293.6 11.7 %cholesky.217 = f32[128,128]{1,0:T(8,128)S(1)} custom-call(f32[128,128]{1,0:T(8,128)S(1)} %cholesky.270), custom_call_target="Cholesky" | custom-call | tf_op jit(solution)/shard_map/jit(cholesky)/cholesky | solution.py:37
  305.4 10.0 %custom-call.28 = f32[1,128,128]{1,2,0:T(8,128)S(1)} custom-call(f32[1,128,128]{2,1,0:T(8,128)S(1)} %get-tuple-element.11), custom_call_target="InvertDiagBlocksLowerTriangular" | custom-call | tf_op jit(solution)/shard_map/jit(cholesky)/cholesky | solution.py:37
  315.6 0.4 convolution_subtract_fusion.1
  316.0 11.7 %cholesky.238 = f32[128,128]{1,0:T(8,128)S(1)} custom-call(f32[128,128]{1,0:T(8,128)S(1)} %cholesky.275), custom_call_target="Cholesky" | custom-call | tf_op jit(solution)/shard_map/jit(cholesky)/cholesky | solution.py:37
  327.8 0.7 compare_reduce_fusion.1
  328.5 9.8 %custom-call.29 = f32[1,128,128]{1,2,0:T(8,128)S(1)} custom-call(f32[1,128,128]{2,1,0:T(8,128)S(1)} %get-tuple-element.8), custom_call_target="InvertDiagBlocksLowerTriangular" | custom-call | tf_op jit(solution)/shard_map/jit(cholesky)/cholesky | solution.py:37
  338.5 0.4 convolution_subtract_fusion.2
  338.9 11.7 %cholesky.255 = f32[128,128]{1,0:T(8,128)S(1)} custom-call(f32[128,128]{1,0:T(8,128)S(1)} %convolution_subtract_fusion.2), custom_call_target="Cholesky" | custom-call | tf_op jit(solution)/shard_map/jit(cholesky)/cholesky | solution.py:37
  350.7 0.6 compare_reduce_fusion
  351.3 0.7 compare_reduce_fusion.2
  354.6 0.7 copy.9
  (19 shorter events, 1.3 us)
Async XLA Ops:
  6.5 0.8 copy-start
  6.5 196.3 %all-reduce.4.cloned.1.call-start = ((), (), s32[]{:S(2)}) async-start(), calls=%async_computation.1 | async-start | bytes 2097152 | tf_op jit(solution)/shard_map/psum | solution.py:6
  55.5 212.3 %all-reduce.6.cloned.1.call-start = ((), (), s32[]{:S(2)}) async-start(), calls=%async_computation.2 | async-start | bytes 2097152 | tf_op jit(solution)/shard_map/psum | solution.py:6
Sparse Core Ops, SparseCore 0:
  55.6 147.1 all-reduce.3
  205.1 62.6 all-reduce.5
